TPU v7x, 512 devices: a whole 4x4x16 slice. The times are simulated.
512 devices in a mesh: sec: 2 (over z_hi), gx: 16 (over z_lo, core), gy: 16 (over x, y).
Axes of the slice: x: 4, y: 4, z: 16 (z_hi: 2, z_lo: 8; z = z_hi * 8 + z_lo), core: 2. Of those that a mesh axis runs over, the one named last changes fastest.
Arguments:
- terminal: float32 [4, 16, 256, 4096], P('sec', None, 'gx', 'gy'), may hold values from -6 to 6
- forward_temp: bfloat16 [2, 4, 16, 256, 4096], P(None, 'sec', None, 'gx', 'gy'), may hold values from -6 to 6
- conductivity: float32 [16, 256, 4096], P(None, 'gx', 'gy'), may hold values from 0.02 to 0.15
- velocity: float32 [2, 16, 256, 4096], P(None, None, 'gx', 'gy'), may hold values from -0.3 to 0.3
- fixed_mask: int32 [16, 256, 4096], P(None, 'gx', 'gy'), may hold values 0 or 1
- wells: int32 [4, 8, 3], P('sec'), may hold values from 0 to 4095, as said below
- misfit: float32 [2, 4, 8], P(None, 'sec'), may hold values from -12 to 12
- head_gradient: bfloat16 [2, 16, 256, 4096], P('sec', None, 'gx', 'gy'), may hold values from -6 to 6
- blocks: bfloat16 [32, 7, 128, 128], P('gy'), may hold values from -0.1875 to 0.1875
- block_cols: int32 [32, 7], P('gy'), may hold values from 0 to 31, as said below
Outputs:
- head_adjoint: float32 [2, 16, 256, 4096], P('sec', None, 'gx', 'gy')
- sensitivity: float32 [16, 256, 4096], P(None, 'gx', 'gy')
Inputs may be any that keep to these rules, and one draw needn't show every extreme that they name: `wells`: each row is one cell (z, x, y) with z < 16, x < 256, y < 4096; the first test observes the cells (0, 0, 0) and (15, 255, 4095). `block_cols`: row r lists 7 different block columns, the first of which is r.
All inputs are finite; a program needn't handle non-finite values. No bound on the sum of `fixed_mask` on one device may be relied on, other than what follows from the above.
Results may differ from a plain program's by a relative error of at most 0.0029.
Values may be sent and summed in bfloat16 or wider, within the bound.
No kernel may reach another device: no remote copies, remote signals or barrier semaphores. Data moves between devices by JAX's collectives and lax.ppermute only.
A program may use at most 64 MiB of HBM per device.

v0:
```python
import jax
import jax.numpy as jnp
from jax import lax
from jax.sharding import PartitionSpec as P


def extended(cells, sides, width):
    for axis, dim in sides:
        count = lax.axis_size(axis)
        ends = count - 1
        head = lax.slice_in_dim(cells, 0, width, axis=dim)
        tail = lax.slice_in_dim(cells, cells.shape[dim] - width, cells.shape[dim], axis=dim)
        cells = jnp.concatenate(
            [
                lax.ppermute(tail, axis, [(i, (i + 1) % count) for i in range(ends)]),
                cells,
                lax.ppermute(head, axis, [((i + 1) % count, i) for i in range(ends)]),
            ],
            axis=dim,
        )
    return cells


def shifted(padded):
    lead = [(0, 0)] * (padded.ndim - 3)
    deeper = jnp.pad(padded, lead + [(1, 1), (0, 0), (0, 0)])
    centre = deeper[..., 1:-1, 1:-1, 1:-1]
    beside_all = [
        deeper[..., 2:, 1:-1, 1:-1],
        deeper[..., :-2, 1:-1, 1:-1],
        deeper[..., 1:-1, 2:, 1:-1],
        deeper[..., 1:-1, :-2, 1:-1],
        deeper[..., 1:-1, 1:-1, 2:],
        deeper[..., 1:-1, 1:-1, :-2],
    ]
    return (centre, beside_all)


def face_weights(kappa_pad):
    centre, beside_all = shifted(kappa_pad)
    return [
        2.0 * centre * other / jnp.where(centre + other > 0.0, centre + other, 1.0)
        for other in beside_all
    ]


def advance(adjoint_pad, weights, keep, speed_x, speed_y, source):
    centre, beside_all = shifted(adjoint_pad)
    diffusion = weights[0] * (beside_all[0] - centre)
    for face in range(1, 6):
        diffusion = diffusion + weights[face] * (beside_all[face] - centre)
    slope_x = 0.5 * (beside_all[2] - beside_all[3])
    slope_y = 0.5 * (beside_all[4] - beside_all[5])
    updated = keep * (centre + diffusion + speed_x * slope_x + speed_y * slope_y + source)
    return (updated, diffusion, slope_x, slope_y)


def well_sources(wells, misfit_level, layers, rows_x, cols_y, margin):
    start_x = lax.axis_index("gx") * rows_x - margin
    start_y = lax.axis_index("gy") * cols_y - margin
    coord_z = jnp.arange(layers, dtype=jnp.int32)[:, None, None]
    coord_x = (start_x + jnp.arange(rows_x + 2 * margin, dtype=jnp.int32))[None, :, None]
    coord_y = (start_y + jnp.arange(cols_y + 2 * margin, dtype=jnp.int32))[None, None, :]
    well_z = wells[:, :, 0][:, :, None, None, None]
    well_x = wells[:, :, 1][:, :, None, None, None]
    well_y = wells[:, :, 2][:, :, None, None, None]
    matches = (coord_z == well_z) & (coord_x == well_x) & (coord_y == well_y)
    return jnp.sum(jnp.where(matches, misfit_level[:, :, None, None, None], 0.0), axis=1)


def shards(
    terminal,
    forward_temp,
    conductivity,
    velocity,
    fixed_mask,
    wells,
    misfit,
    head_gradient,
    blocks,
    block_cols,
):
    layers, rows_x, cols_y = conductivity.shape
    steps = forward_temp.shape[0]
    keep = 1.0 - fixed_mask.astype(jnp.float32)
    heat_sens = jnp.zeros((layers, rows_x, cols_y), jnp.float32)
    flow_x = jnp.zeros((layers, rows_x, cols_y), jnp.float32)
    flow_y = jnp.zeros((layers, rows_x, cols_y), jnp.float32)
    kappa_pad = extended(conductivity, (("gx", 1), ("gy", 2)), 1)
    weights = face_weights(kappa_pad)
    adjoint = terminal
    for level in reversed(range(steps)):
        padded = extended(adjoint, (("gx", 2), ("gy", 3)), 1)
        source = well_sources(wells, misfit[level], layers, rows_x, cols_y, 0)
        adjoint, diffusion, slope_x, slope_y = advance(
            padded, weights, keep, velocity[0], velocity[1], source
        )
        temper = forward_temp[level].astype(jnp.float32)
        heat_sens = heat_sens + jnp.sum(temper * diffusion, axis=0)
        flow_x = flow_x + jnp.sum(temper * slope_x, axis=0)
        flow_y = flow_y + jnp.sum(temper * slope_y, axis=0)
    first = lax.axis_index("sec") == 0
    mine = jnp.where(first, flow_x, flow_y)
    other = jnp.where(first, flow_y, flow_x)
    partner = [(0, 1), (1, 0)]
    rounded = (mine + lax.ppermute(other, "sec", partner)).astype(jnp.bfloat16)
    row_blocks, per_row, block_size, _ = blocks.shape
    piece = lax.all_gather(rounded, "gy", axis=2, tiled=True)
    count = piece.shape[2] // block_size
    split_rows = piece.reshape(layers, rows_x, count, block_size)
    block_ids = jnp.arange(count, dtype=jnp.int32)
    chosen = (block_cols[:, :, None] == block_ids[None, None, :]).astype(jnp.bfloat16)
    portion = jnp.einsum("bkq,zxqj->bkzxj", chosen, split_rows, preferred_element_type=jnp.float32)
    picked = portion.astype(jnp.bfloat16)
    head = jnp.einsum(
        "bkzxj,bkij->zxbi", picked, blocks, preferred_element_type=jnp.float32
    ).reshape(layers, rows_x, cols_y)
    partial_sens = heat_sens + head * head_gradient[0].astype(jnp.float32)
    sensitivity = partial_sens + lax.ppermute(partial_sens, "sec", partner)
    return (head[None], sensitivity)


def solution(mesh):
    placed = (
        P("sec", None, "gx", "gy"),
        P(None, "sec", None, "gx", "gy"),
        P(None, "gx", "gy"),
        P(None, None, "gx", "gy"),
        P(None, "gx", "gy"),
        P("sec", None, None),
        P(None, "sec", None),
        P("sec", None, "gx", "gy"),
        P("gy", None, None, None),
        P("gy", None),
    )
    return jax.shard_map(
        shards,
        mesh=mesh,
        in_specs=placed,
        out_specs=(P("sec", None, "gx", "gy"), P(None, "gx", "gy")),
        check_vma=False,
    )
```

profile of v0, /device:TPU:32, one launch (start us, length us, event | category | flops | bytes accessed | tf_op | source)
XLA Modules:
  0.0 226.1 jit_solution(11138354482306704369)
XLA Ops:
  7.3 1.1 fusion.57
  8.3 1.9 collective-permute-start.2
  10.2 3.6 %collective-permute-start.3 = (f32[16,1,256]{2,1,0:T(1,128)S(1)}, f32[16,1,256]{2,1,0:T(1,128)S(1)}, u32[]{:S(2)}, u32[]{:S(2)}) collective-permute-start(f32[16,1,256]{2,1,0:T(1,128)S(1)} %get-tuple-element.30), channel_id=1, source_target_pairs={{16,0},{32,16},{48,32},{64,48},{80,64},{96,80},{112,96},{128,112},... | collective-permute-start | bytes 49160 | tf_op jit(solution)/shard_map/ppermute | solution.py:17
  13.9 1.1 fusion.55
  15.0 5.1 %collective-permute-start = (f32[2,16,1,256]{3,2,1,0:T(1,128)S(1)}, f32[2,16,1,256]{3,2,1,0:T(1,128)S(1)}, u32[]{:S(2)}, u32[]{:S(2)}) collective-permute-start(f32[2,16,1,256]{3,2,1,0:T(1,128)S(1)} %get-tuple-element.19), channel_id=1, source_target_pairs={{16,0},{32,16},{48,32},{64,48},{80,64},{96,80},{112,96},{128,112},... | collective-permute-start | bytes 98312 | tf_op jit(solution)/shard_map/ppermute | solution.py:17
  20.1 1.9 collective-permute-start.1
  22.8 1.1 multiply_bitcast_fusion.1
  24.4 1.4 collective-permute-start.4
  25.8 1.3 collective-permute-start.5
  28.0 3.1 %collective-permute-done.4 = f32[16,18,1]{2,1,0:T(8,128)S(1)} collective-permute-done((f32[16,18,1]{2,1,0:T(8,128)S(1)}, f32[16,18,1]{2,1,0:T(8,128)S(1)}, u32[]{:S(2)}, u32[]{:S(2)}) %collective-permute-start.4) | collective-permute-done | bytes 1184 | tf_op jit(solution)/shard_map/ppermute | solution.py:15
  31.1 4.2 %collective-permute-done.5 = f32[16,18,1]{2,1,0:T(8,128)S(1)} collective-permute-done((f32[16,18,1]{2,1,0:T(8,128)S(1)}, f32[16,18,1]{2,1,0:T(8,128)S(1)}, u32[]{:S(2)}, u32[]{:S(2)}) %collective-permute-start.5) | collective-permute-done | bytes 1184 | tf_op jit(solution)/shard_map/ppermute | solution.py:17
  36.0 2.9 %collective-permute-start.6 = (f32[2,16,18,1]{3,2,1,0:T(8,128)S(1)}, f32[2,16,18,1]{3,2,1,0:T(8,128)S(1)}, u32[]{:S(2)}, u32[]{:S(2)}) collective-permute-start(f32[2,16,18,1]{3,2,1,0:T(8,128)S(1)} %get-tuple-element.14), channel_id=1, source_target_pairs={{0,1},{1,2},{2,3},{3,4},{4,5},{5,6},{6,7},{7,8},{8,9},{9,10},{10,1... | collective-permute-start | bytes 6920 | tf_op jit(solution)/shard_map/ppermute | solution.py:15
  38.9 1.3 collective-permute-start.7
  40.8 6.7 %collective-permute-done.6 = f32[2,16,18,1]{3,2,1,0:T(8,128)S(1)} collective-permute-done((f32[2,16,18,1]{3,2,1,0:T(8,128)S(1)}, f32[2,16,18,1]{3,2,1,0:T(8,128)S(1)}, u32[]{:S(2)}, u32[]{:S(2)}) %collective-permute-start.6) | collective-permute-done | bytes 2336 | tf_op jit(solution)/shard_map/ppermute | solution.py:15
  47.5 4.1 %collective-permute-done.7 = f32[2,16,18,1]{3,2,1,0:T(8,128)S(1)} collective-permute-done((f32[2,16,18,1]{3,2,1,0:T(8,128)S(1)}, f32[2,16,18,1]{3,2,1,0:T(8,128)S(1)}, u32[]{:S(2)}, u32[]{:S(2)}) %collective-permute-start.7) | collective-permute-done | bytes 2336 | tf_op jit(solution)/shard_map/ppermute | solution.py:17
  52.4 1.8 add_multiply_fusion
  54.3 1.9 collective-permute-start.8
  56.2 2.4 %collective-permute-start.9 = (f32[2,16,1,256]{3,2,1,0:T(1,128)S(1)}, f32[2,16,1,256]{3,2,1,0:T(1,128)S(1)}, u32[]{:S(2)}, u32[]{:S(2)}) collective-permute-start(f32[2,16,1,256]{3,2,1,0:T(1,128)S(1)} %get-tuple-element.16), channel_id=1, source_target_pairs={{0,16},{16,32},{32,48},{48,64},{64,80},{80,96},{96,112},{112,128},... | collective-permute-start | bytes 98312 | tf_op jit(solution)/shard_map/ppermute | solution.py:15
  58.7 2.8 %collective-permute-done.9 = f32[2,16,1,256]{3,2,1,0:T(1,128)S(1)} collective-permute-done((f32[2,16,1,256]{3,2,1,0:T(1,128)S(1)}, f32[2,16,1,256]{3,2,1,0:T(1,128)S(1)}, u32[]{:S(2)}, u32[]{:S(2)}) %collective-permute-start.9) | collective-permute-done | bytes 32800 | tf_op jit(solution)/shard_map/ppermute | solution.py:15
  61.8 1.4 collective-permute-start.10
  63.2 5.3 %collective-permute-start.11 = (f32[2,16,18,1]{3,2,1,0:T(8,128)S(1)}, f32[2,16,18,1]{3,2,1,0:T(8,128)S(1)}, u32[]{:S(2)}, u32[]{:S(2)}) collective-permute-start(f32[2,16,18,1]{3,2,1,0:T(8,128)S(1)} %get-tuple-element.12), channel_id=1, source_target_pairs={{0,1},{1,2},{2,3},{3,4},{4,5},{5,6},{6,7},{7,8},{8,9},{9,10},{10,1... | collective-permute-start | bytes 6920 | tf_op jit(solution)/shard_map/ppermute | solution.py:15
  69.1 6.4 %collective-permute-done.10 = f32[2,16,18,1]{3,2,1,0:T(8,128)S(1)} collective-permute-done((f32[2,16,18,1]{3,2,1,0:T(8,128)S(1)}, f32[2,16,18,1]{3,2,1,0:T(8,128)S(1)}, u32[]{:S(2)}, u32[]{:S(2)}) %collective-permute-start.10) | collective-permute-done | bytes 2336 | tf_op jit(solution)/shard_map/ppermute | solution.py:17
  75.6 1.2 collective-permute-done.11
  76.8 1.3 fusion.7
  78.2 13.0 %collective-permute-start.12 = (f32[16,16,256]{2,1,0:T(8,128)S(1)}, f32[16,16,256]{2,1,0:T(8,128)S(1)}, u32[]{:S(2)}, u32[]{:S(2)}) collective-permute-start(f32[16,16,256]{2,1,0:T(8,128)S(1)} %broadcast_select_fusion), channel_id=1, source_target_pairs={{0,256},{256,0},{1,257},{257,1},{2,258},{258,2},{3,259},{259,3},{4... | collective-permute-start | bytes 786440 | tf_op jit(solution)/shard_map/ppermute | solution.py:106
  91.2 10.4 %collective-permute-done.12 = f32[16,16,256]{2,1,0:T(8,128)S(1)} collective-permute-done((f32[16,16,256]{2,1,0:T(8,128)S(1)}, f32[16,16,256]{2,1,0:T(8,128)S(1)}, u32[]{:S(2)}, u32[]{:S(2)}) %collective-permute-start.12) | collective-permute-done | bytes 262176 | tf_op jit(solution)/shard_map/ppermute | solution.py:106
  103.8 1.7 fusion.9
  105.5 76.5 %all-gather.2.cloned.1.call-done = bf16[16,16,4096]{2,1,0:T(8,128)(2,1)} async-done(((bf16[16,16,256]{2,1,0:T(8,128)(2,1)}), bf16[16,16,4096]{2,1,0:T(8,128)(2,1)}) %all-gather.2.cloned.1.call-update) | async-done | bytes 2097168 | tf_op jit(solution)/shard_map/all_gather | solution.py:108
  181.9 2.1 copy.21
  185.7 11.9 %collective-permute-start.13 = (f32[16,16,256]{2,1,0:T(8,128)S(1)}, f32[16,16,256]{2,1,0:T(8,128)S(1)}, u32[]{:S(2)}, u32[]{:S(2)}) collective-permute-start(f32[16,16,256]{2,1,0:T(8,128)S(1)} %fusion.43), channel_id=1, source_target_pairs={{0,256},{256,0},{1,257},{257,1},{2,258},{258,2},{3,259},{259,3},{4... | collective-permute-start | bytes 786440 | tf_op jit(solution)/shard_map/ppermute | solution.py:119
  197.8 0.9 broadcast_in_dim_reshape.3
  198.7 19.8 %collective-permute-done.13 = f32[16,16,256]{2,1,0:T(8,128)S(1)} collective-permute-done((f32[16,16,256]{2,1,0:T(8,128)S(1)}, f32[16,16,256]{2,1,0:T(8,128)S(1)}, u32[]{:S(2)}, u32[]{:S(2)}) %collective-permute-start.13) | collective-permute-done | bytes 262176 | tf_op jit(solution)/shard_map/ppermute | solution.py:119
  (79 shorter events, 9.8 us)
Async XLA Ops:
  7.2 177.4 %copy-start = (bf16[2,7,128,128]{3,2,1,0:T(8,128)(2,1)S(1)}, bf16[2,7,128,128]{3,2,1,0:T(8,128)(2,1)}, u32[]{:S(2)}) copy-start(bf16[2,7,128,128]{3,2,1,0:T(8,128)(2,1)} %param.18) | copy-start | bytes 1376260
  7.2 17.0 %copy-start.2 = (f32[16,16,256]{2,1,0:T(8,128)S(1)}, f32[16,16,256]{2,1,0:T(8,128)}, u32[]{:S(2)}) copy-start(f32[16,16,256]{2,1,0:T(8,128)} %param.12) | copy-start | bytes 786436
  7.2 16.7 %copy-start.18 = (s32[16,16,256]{2,1,0:T(8,128)S(1)}, s32[16,16,256]{2,1,0:T(8,128)}, u32[]{:S(2)}) copy-start(s32[16,16,256]{2,1,0:T(8,128)} %param.14) | copy-start | bytes 786436
  7.2 17.0 %copy-start.21 = (f32[2,2,8]{2,1,0:T(2,128)S(1)}, f32[2,2,8]{2,1,0:T(2,128)}, u32[]{:S(2)}) copy-start(f32[2,2,8]{2,1,0:T(2,128)} %param.16) | copy-start | bytes 388
  7.2 174.7 %all-gather.2.cloned.1.call-start = ((), (), s32[]{:S(2)}) async-start(), calls=%async_computation | async-start | bytes 2228224 | tf_op jit(solution)/shard_map/all_gather | solution.py:108
  8.3 15.9 %collective-permute-start.2 = (f32[16,1,256]{2,1,0:T(1,128)S(1)}, f32[16,1,256]{2,1,0:T(1,128)S(1)}, u32[]{:S(2)}, u32[]{:S(2)}) collective-permute-start(f32[16,1,256]{2,1,0:T(1,128)S(1)} %get-tuple-element.29), channel_id=1, source_target_pairs={{0,16},{16,32},{32,48},{48,64},{64,80},{80,96},{96,112},{112,128},... | collective-permute-start | bytes 49160 | tf_op jit(solution)/shard_map/ppermute | solution.py:15
  10.2 13.9 %collective-permute-start.3 = (f32[16,1,256]{2,1,0:T(1,128)S(1)}, f32[16,1,256]{2,1,0:T(1,128)S(1)}, u32[]{:S(2)}, u32[]{:S(2)}) collective-permute-start(f32[16,1,256]{2,1,0:T(1,128)S(1)} %get-tuple-element.30), channel_id=1, source_target_pairs={{16,0},{32,16},{48,32},{64,48},{80,64},{96,80},{112,96},{128,112},... | collective-permute-start | bytes 49160 | tf_op jit(solution)/shard_map/ppermute | solution.py:17
  15.0 20.7 %collective-permute-start = (f32[2,16,1,256]{3,2,1,0:T(1,128)S(1)}, f32[2,16,1,256]{3,2,1,0:T(1,128)S(1)}, u32[]{:S(2)}, u32[]{:S(2)}) collective-permute-start(f32[2,16,1,256]{3,2,1,0:T(1,128)S(1)} %get-tuple-element.19), channel_id=1, source_target_pairs={{16,0},{32,16},{48,32},{64,48},{80,64},{96,80},{112,96},{128,112},... | collective-permute-start | bytes 98312 | tf_op jit(solution)/shard_map/ppermute | solution.py:17
  20.1 15.5 %collective-permute-start.1 = (f32[2,16,1,256]{3,2,1,0:T(1,128)S(1)}, f32[2,16,1,256]{3,2,1,0:T(1,128)S(1)}, u32[]{:S(2)}, u32[]{:S(2)}) collective-permute-start(f32[2,16,1,256]{3,2,1,0:T(1,128)S(1)} %get-tuple-element.20), channel_id=1, source_target_pairs={{0,16},{16,32},{32,48},{48,64},{64,80},{80,96},{96,112},{112,128},... | collective-permute-start | bytes 98312 | tf_op jit(solution)/shard_map/ppermute | solution.py:15
  24.3 11.4 %copy-start.1 = (f32[2,16,16,256]{3,2,1,0:T(8,128)S(1)}, f32[2,16,16,256]{3,2,1,0:T(8,128)}, u32[]{:S(2)}) copy-start(f32[2,16,16,256]{3,2,1,0:T(8,128)} %param.10) | copy-start | bytes 1572868
  24.4 6.7 %collective-permute-start.4 = (f32[16,18,1]{2,1,0:T(8,128)S(1)}, f32[16,18,1]{2,1,0:T(8,128)S(1)}, u32[]{:S(2)}, u32[]{:S(2)}) collective-permute-start(f32[16,18,1]{2,1,0:T(8,128)S(1)} %get-tuple-element.22), channel_id=1, source_target_pairs={{0,1},{1,2},{2,3},{3,4},{4,5},{5,6},{6,7},{7,8},{8,9},{9,10},{10,1... | collective-permute-start | bytes 3464 | tf_op jit(solution)/shard_map/ppermute | solution.py:15
  25.8 9.4 %collective-permute-start.5 = (f32[16,18,1]{2,1,0:T(8,128)S(1)}, f32[16,18,1]{2,1,0:T(8,128)S(1)}, u32[]{:S(2)}, u32[]{:S(2)}) collective-permute-start(f32[16,18,1]{2,1,0:T(8,128)S(1)} %get-tuple-element.21), channel_id=1, source_target_pairs={{1,0},{2,1},{3,2},{4,3},{5,4},{6,5},{7,6},{8,7},{9,8},{10,9},{11,1... | collective-permute-start | bytes 3464 | tf_op jit(solution)/shard_map/ppermute | solution.py:17
  36.0 11.5 %collective-permute-start.6 = (f32[2,16,18,1]{3,2,1,0:T(8,128)S(1)}, f32[2,16,18,1]{3,2,1,0:T(8,128)S(1)}, u32[]{:S(2)}, u32[]{:S(2)}) collective-permute-start(f32[2,16,18,1]{3,2,1,0:T(8,128)S(1)} %get-tuple-element.14), channel_id=1, source_target_pairs={{0,1},{1,2},{2,3},{3,4},{4,5},{5,6},{6,7},{7,8},{8,9},{9,10},{10,1... | collective-permute-start | bytes 6920 | tf_op jit(solution)/shard_map/ppermute | solution.py:15
  38.9 12.7 %collective-permute-start.7 = (f32[2,16,18,1]{3,2,1,0:T(8,128)S(1)}, f32[2,16,18,1]{3,2,1,0:T(8,128)S(1)}, u32[]{:S(2)}, u32[]{:S(2)}) collective-permute-start(f32[2,16,18,1]{3,2,1,0:T(8,128)S(1)} %get-tuple-element.13), channel_id=1, source_target_pairs={{1,0},{2,1},{3,2},{4,3},{5,4},{6,5},{7,6},{8,7},{9,8},{10,9},{11,1... | collective-permute-start | bytes 6920 | tf_op jit(solution)/shard_map/ppermute | solution.py:17
  40.8 11.6 %copy-start.3 = (f32[16,16,256]{2,1,0:T(8,128)}, f32[16,16,256]{2,1,0:T(8,128)S(1)}, u32[]{:S(2)}) copy-start(f32[16,16,256]{2,1,0:T(8,128)S(1)} %get-tuple-element.24) | copy-start | bytes 786436
  40.8 11.6 %copy-start.5 = (f32[16,16,256]{2,1,0:T(8,128)}, f32[16,16,256]{2,1,0:T(8,128)S(1)}, u32[]{:S(2)}) copy-start(f32[16,16,256]{2,1,0:T(8,128)S(1)} %get-tuple-element.25) | copy-start | bytes 786436
  40.8 11.6 %copy-start.7 = (f32[16,16,256]{2,1,0:T(8,128)}, f32[16,16,256]{2,1,0:T(8,128)S(1)}, u32[]{:S(2)}) copy-start(f32[16,16,256]{2,1,0:T(8,128)S(1)} %get-tuple-element.26) | copy-start | bytes 786436
  40.8 11.6 %copy-start.9 = (f32[16,16,256]{2,1,0:T(8,128)}, f32[16,16,256]{2,1,0:T(8,128)S(1)}, u32[]{:S(2)}) copy-start(f32[16,16,256]{2,1,0:T(8,128)S(1)} %get-tuple-element.27) | copy-start | bytes 786436
  40.8 11.6 %copy-start.11 = (f32[16,16,256]{2,1,0:T(8,128)}, f32[16,16,256]{2,1,0:T(8,128)S(1)}, u32[]{:S(2)}) copy-start(f32[16,16,256]{2,1,0:T(8,128)S(1)} %get-tuple-element.28) | copy-start | bytes 786436
  54.3 4.4 %collective-permute-start.8 = (f32[2,16,1,256]{3,2,1,0:T(1,128)S(1)}, f32[2,16,1,256]{3,2,1,0:T(1,128)S(1)}, u32[]{:S(2)}, u32[]{:S(2)}) collective-permute-start(f32[2,16,1,256]{3,2,1,0:T(1,128)S(1)} %get-tuple-element.15), channel_id=1, source_target_pairs={{16,0},{32,16},{48,32},{64,48},{80,64},{96,80},{112,96},{128,112},... | collective-permute-start | bytes 98312 | tf_op jit(solution)/shard_map/ppermute | solution.py:17
  56.2 5.2 %collective-permute-start.9 = (f32[2,16,1,256]{3,2,1,0:T(1,128)S(1)}, f32[2,16,1,256]{3,2,1,0:T(1,128)S(1)}, u32[]{:S(2)}, u32[]{:S(2)}) collective-permute-start(f32[2,16,1,256]{3,2,1,0:T(1,128)S(1)} %get-tuple-element.16), channel_id=1, source_target_pairs={{0,16},{16,32},{32,48},{48,64},{64,80},{80,96},{96,112},{112,128},... | collective-permute-start | bytes 98312 | tf_op jit(solution)/shard_map/ppermute | solution.py:15
  58.7 9.9 %copy-start.13 = (bf16[2,2,16,16,256]{4,3,2,1,0:T(8,128)(2,1)S(1)}, bf16[2,2,16,16,256]{4,3,2,1,0:T(8,128)(2,1)}, u32[]{:S(2)}) copy-start(bf16[2,2,16,16,256]{4,3,2,1,0:T(8,128)(2,1)} %param.11) | copy-start | bytes 1572868
  61.8 15.0 %copy-start.15 = (f32[2,16,16,256]{3,2,1,0:T(8,128)S(1)}, f32[2,16,16,256]{3,2,1,0:T(8,128)}, u32[]{:S(2)}) copy-start(f32[2,16,16,256]{3,2,1,0:T(8,128)} %get-tuple-element.8) | copy-start | bytes 1572868
  61.8 13.8 %collective-permute-start.10 = (f32[2,16,18,1]{3,2,1,0:T(8,128)S(1)}, f32[2,16,18,1]{3,2,1,0:T(8,128)S(1)}, u32[]{:S(2)}, u32[]{:S(2)}) collective-permute-start(f32[2,16,18,1]{3,2,1,0:T(8,128)S(1)} %get-tuple-element.11), channel_id=1, source_target_pairs={{1,0},{2,1},{3,2},{4,3},{5,4},{6,5},{7,6},{8,7},{9,8},{10,9},{11,1... | collective-permute-start | bytes 6920 | tf_op jit(solution)/shard_map/ppermute | solution.py:17
  63.2 13.6 %collective-permute-start.11 = (f32[2,16,18,1]{3,2,1,0:T(8,128)S(1)}, f32[2,16,18,1]{3,2,1,0:T(8,128)S(1)}, u32[]{:S(2)}, u32[]{:S(2)}) collective-permute-start(f32[2,16,18,1]{3,2,1,0:T(8,128)S(1)} %get-tuple-element.12), channel_id=1, source_target_pairs={{0,1},{1,2},{2,3},{3,4},{4,5},{5,6},{6,7},{7,8},{8,9},{9,10},{10,1... | collective-permute-start | bytes 6920 | tf_op jit(solution)/shard_map/ppermute | solution.py:15
  78.2 23.4 %collective-permute-start.12 = (f32[16,16,256]{2,1,0:T(8,128)S(1)}, f32[16,16,256]{2,1,0:T(8,128)S(1)}, u32[]{:S(2)}, u32[]{:S(2)}) collective-permute-start(f32[16,16,256]{2,1,0:T(8,128)S(1)} %broadcast_select_fusion), channel_id=1, source_target_pairs={{0,256},{256,0},{1,257},{257,1},{2,258},{258,2},{3,259},{259,3},{4... | collective-permute-start | bytes 786440 | tf_op jit(solution)/shard_map/ppermute | solution.py:106
  102.4 1.1 copy-start.8
  102.4 1.2 copy-start.10
  102.4 1.2 copy-start.12
  102.4 1.4 copy-start.14
  181.9 2.1 copy-start.20
  185.7 32.8 %collective-permute-start.13 = (f32[16,16,256]{2,1,0:T(8,128)S(1)}, f32[16,16,256]{2,1,0:T(8,128)S(1)}, u32[]{:S(2)}, u32[]{:S(2)}) collective-permute-start(f32[16,16,256]{2,1,0:T(8,128)S(1)} %fusion.43), channel_id=1, source_target_pairs={{0,256},{256,0},{1,257},{257,1},{2,258},{258,2},{3,259},{259,3},{4... | collective-permute-start | bytes 786440 | tf_op jit(solution)/shard_map/ppermute | solution.py:119
  (5 other events, 5.0 us)
Sparse Core Ops, SparseCore 0:
  102.5 79.4 all-gather.1
where the time goes:
time: 227 us; the launch traced here: 226 us
  waiting for transfers between devices  135 us (59%)
  starting transfers between devices  55.7 us (25%)
  between operations  14.6 us (6%)
  other arithmetic  11.9 us (5%)
  local copies, waits for them, and re-layouts  7.91 us (3%)
    all_gather x1, waiting for transfers between devices, shards(): piece = lax.all_gather(rounded, 'gy', axis=2, tiled=True)  76.5 us
    ppermute x1, waiting for transfers between devices, shards(): sensitivity = partial_sens + lax.ppermute(partial_sens, 'sec', partner)  19.8 us
    ppermute x6, starting transfers between devices, extended(): lax.ppermute(tail, axis, [(i, (i + 1) % count) for i in range(ends)])  16 us
    ppermute x6, waiting for transfers between devices, extended(): lax.ppermute(head, axis, [((i + 1) % count, i) for i in range(ends)])  14.7 us
    ppermute x6, starting transfers between devices, extended(): lax.ppermute(head, axis, [((i + 1) % count, i) for i in range(ends)])  14.7 us
    ppermute x6, waiting for transfers between devices, extended(): lax.ppermute(tail, axis, [(i, (i + 1) % count) for i in range(ends)])  13.8 us
    ppermute x1, starting transfers between devices, shards(): rounded = (mine + lax.ppermute(other, 'sec', partner)).astype(jnp.bfloat16)  13 us
    ppermute x1, starting transfers between devices, shards(): sensitivity = partial_sens + lax.ppermute(partial_sens, 'sec', partner)  11.9 us
  transfers between devices with their start and end apart: 15, of which 10 were waited for; matrix products, arithmetic and copies ran while one was open for 4% of the time, Pallas kernels for 0%

commit v1 on v0

--- a/solution.py
+++ b/solution.py
@@ -105,7 +105,9 @@
     partner = [(0, 1), (1, 0)]
     rounded = (mine + lax.ppermute(other, "sec", partner)).astype(jnp.bfloat16)
     row_blocks, per_row, block_size, _ = blocks.shape
-    piece = lax.all_gather(rounded, "gy", axis=2, tiled=True)
+    piece = jnp.concatenate(
+        lax.all_to_all(jnp.stack([rounded] * lax.axis_size("gy")), "gy", 0, 0), axis=2
+    )
     count = piece.shape[2] // block_size
     split_rows = piece.reshape(layers, rows_x, count, block_size)
     block_ids = jnp.arange(count, dtype=jnp.int32)

time: 227 us -> 181 us (0.80)
  the two profiles are of different devices: /device:TPU:32 before, /device:TPU:83 now
where the time goes in v1:
time: 181 us; the launch traced here: 180 us
  waiting for transfers between devices  83.7 us (46%)
  starting transfers between devices  69.5 us (38%)
  other arithmetic  12.5 us (7%)
  local copies, waits for them, and re-layouts  12 us (7%)
    ppermute x6, starting transfers between devices, extended(): lax.ppermute(tail, axis, [(i, (i + 1) % count) for i in range(ends)])  22.8 us
    all_to_all x1, waiting for transfers between devices, shards(): lax.all_to_all(jnp.stack([rounded] * lax.axis_size('gy')), 'gy', 0, 0)  22.2 us
    ppermute x1, waiting for transfers between devices, shards(): rounded = (mine + lax.ppermute(other, 'sec', partner)).astype(jnp.bfloat16)  22.2 us
    ppermute x1, waiting for transfers between devices, shards(): sensitivity = partial_sens + lax.ppermute(partial_sens, 'sec', partner)  16.2 us
    ppermute x6, starting transfers between devices, extended(): lax.ppermute(head, axis, [((i + 1) % count, i) for i in range(ends)])  13.8 us
    ppermute x6, waiting for transfers between devices, extended(): lax.ppermute(head, axis, [((i + 1) % count, i) for i in range(ends)])  12.7 us
    ppermute x1, starting transfers between devices, shards(): rounded = (mine + lax.ppermute(other, 'sec', partner)).astype(jnp.bfloat16)  12.2 us
    ppermute x1, starting transfers between devices, shards(): sensitivity = partial_sens + lax.ppermute(partial_sens, 'sec', partner)  11 us
  transfers between devices with their start and end apart: 15, of which 10 were waited for; matrix products, arithmetic and copies ran while one was open for 6% of the time, Pallas kernels for 0%

profile of v1, /device:TPU:83, one launch (start us, length us, event | category | flops | bytes accessed | tf_op | source)
XLA Modules:
  0.0 179.8 jit_solution(7508692110517991540)
XLA Ops:
  1.7 4.1 %collective-permute-start.2 = (f32[16,1,256]{2,1,0:T(1,128)S(1)}, f32[16,1,256]{2,1,0:T(1,128)S(1)}, u32[]{:S(2)}, u32[]{:S(2)}) collective-permute-start(f32[16,1,256]{2,1,0:T(1,128)S(1)} %get-tuple-element.29), channel_id=1, source_target_pairs={{0,16},{16,32},{32,48},{48,64},{64,80},{80,96},{96,112},{112,128},... | collective-permute-start | bytes 49160 | tf_op jit(solution)/shard_map/ppermute | solution.py:15
  5.9 1.9 %collective-permute-start.3 = (f32[16,1,256]{2,1,0:T(1,128)S(1)}, f32[16,1,256]{2,1,0:T(1,128)S(1)}, u32[]{:S(2)}, u32[]{:S(2)}) collective-permute-start(f32[16,1,256]{2,1,0:T(1,128)S(1)} %get-tuple-element.30), channel_id=1, source_target_pairs={{16,0},{32,16},{48,32},{64,48},{80,64},{96,80},{112,96},{128,112},... | collective-permute-start | bytes 49160 | tf_op jit(solution)/shard_map/ppermute | solution.py:17
  7.8 1.1 fusion.55
  8.9 2.1 %collective-permute-start = (f32[2,16,1,256]{3,2,1,0:T(1,128)S(1)}, f32[2,16,1,256]{3,2,1,0:T(1,128)S(1)}, u32[]{:S(2)}, u32[]{:S(2)}) collective-permute-start(f32[2,16,1,256]{3,2,1,0:T(1,128)S(1)} %get-tuple-element.19), channel_id=1, source_target_pairs={{16,0},{32,16},{48,32},{64,48},{80,64},{96,80},{112,96},{128,112},... | collective-permute-start | bytes 98312 | tf_op jit(solution)/shard_map/ppermute | solution.py:17
  11.0 3.4 %collective-permute-start.1 = (f32[2,16,1,256]{3,2,1,0:T(1,128)S(1)}, f32[2,16,1,256]{3,2,1,0:T(1,128)S(1)}, u32[]{:S(2)}, u32[]{:S(2)}) collective-permute-start(f32[2,16,1,256]{3,2,1,0:T(1,128)S(1)} %get-tuple-element.20), channel_id=1, source_target_pairs={{0,16},{16,32},{32,48},{48,64},{64,80},{80,96},{96,112},{112,128},... | collective-permute-start | bytes 98312 | tf_op jit(solution)/shard_map/ppermute | solution.py:15
  16.8 3.0 %collective-permute-start.4 = (f32[16,18,1]{2,1,0:T(8,128)S(1)}, f32[16,18,1]{2,1,0:T(8,128)S(1)}, u32[]{:S(2)}, u32[]{:S(2)}) collective-permute-start(f32[16,18,1]{2,1,0:T(8,128)S(1)} %get-tuple-element.22), channel_id=1, source_target_pairs={{0,1},{1,2},{2,3},{3,4},{4,5},{5,6},{6,7},{7,8},{8,9},{9,10},{10,1... | collective-permute-start | bytes 3464 | tf_op jit(solution)/shard_map/ppermute | solution.py:15
  19.8 2.4 %collective-permute-start.5 = (f32[16,18,1]{2,1,0:T(8,128)S(1)}, f32[16,18,1]{2,1,0:T(8,128)S(1)}, u32[]{:S(2)}, u32[]{:S(2)}) collective-permute-start(f32[16,18,1]{2,1,0:T(8,128)S(1)} %get-tuple-element.21), channel_id=1, source_target_pairs={{1,0},{2,1},{3,2},{4,3},{5,4},{6,5},{7,6},{8,7},{9,8},{10,9},{11,1... | collective-permute-start | bytes 3464 | tf_op jit(solution)/shard_map/ppermute | solution.py:17
  23.1 2.1 %collective-permute-done.4 = f32[16,18,1]{2,1,0:T(8,128)S(1)} collective-permute-done((f32[16,18,1]{2,1,0:T(8,128)S(1)}, f32[16,18,1]{2,1,0:T(8,128)S(1)}, u32[]{:S(2)}, u32[]{:S(2)}) %collective-permute-start.4) | collective-permute-done | bytes 1184 | tf_op jit(solution)/shard_map/ppermute | solution.py:15
  25.2 2.9 %collective-permute-done.5 = f32[16,18,1]{2,1,0:T(8,128)S(1)} collective-permute-done((f32[16,18,1]{2,1,0:T(8,128)S(1)}, f32[16,18,1]{2,1,0:T(8,128)S(1)}, u32[]{:S(2)}, u32[]{:S(2)}) %collective-permute-start.5) | collective-permute-done | bytes 1184 | tf_op jit(solution)/shard_map/ppermute | solution.py:17
  28.8 4.9 %collective-permute-start.6 = (f32[2,16,18,1]{3,2,1,0:T(8,128)S(1)}, f32[2,16,18,1]{3,2,1,0:T(8,128)S(1)}, u32[]{:S(2)}, u32[]{:S(2)}) collective-permute-start(f32[2,16,18,1]{3,2,1,0:T(8,128)S(1)} %get-tuple-element.14), channel_id=1, source_target_pairs={{0,1},{1,2},{2,3},{3,4},{4,5},{5,6},{6,7},{7,8},{8,9},{9,10},{10,1... | collective-permute-start | bytes 6920 | tf_op jit(solution)/shard_map/ppermute | solution.py:15
  33.7 1.9 %collective-permute-start.7 = (f32[2,16,18,1]{3,2,1,0:T(8,128)S(1)}, f32[2,16,18,1]{3,2,1,0:T(8,128)S(1)}, u32[]{:S(2)}, u32[]{:S(2)}) collective-permute-start(f32[2,16,18,1]{3,2,1,0:T(8,128)S(1)} %get-tuple-element.13), channel_id=1, source_target_pairs={{1,0},{2,1},{3,2},{4,3},{5,4},{6,5},{7,6},{8,7},{9,8},{10,9},{11,1... | collective-permute-start | bytes 6920 | tf_op jit(solution)/shard_map/ppermute | solution.py:17
  36.3 5.5 %collective-permute-done.6 = f32[2,16,18,1]{3,2,1,0:T(8,128)S(1)} collective-permute-done((f32[2,16,18,1]{3,2,1,0:T(8,128)S(1)}, f32[2,16,18,1]{3,2,1,0:T(8,128)S(1)}, u32[]{:S(2)}, u32[]{:S(2)}) %collective-permute-start.6) | collective-permute-done | bytes 2336 | tf_op jit(solution)/shard_map/ppermute | solution.py:15
  41.8 3.8 %collective-permute-done.7 = f32[2,16,18,1]{3,2,1,0:T(8,128)S(1)} collective-permute-done((f32[2,16,18,1]{3,2,1,0:T(8,128)S(1)}, f32[2,16,18,1]{3,2,1,0:T(8,128)S(1)}, u32[]{:S(2)}, u32[]{:S(2)}) %collective-permute-start.7) | collective-permute-done | bytes 2336 | tf_op jit(solution)/shard_map/ppermute | solution.py:17
  46.4 1.8 %add_multiply_fusion = (f32[2,16,16,256]{3,2,1,0:T(8,128)S(1)}, f32[2,16,16,256]{3,2,1,0:T(8,128)}) fusion(f32[2,16,16,256]{3,2,1,0:T(8,128)S(1)} %select_reduce_fusion, f32[2,16,16,256]{3,2,1,0:T(8,128)S(1)} %copy-done.1, f32[2,16,1,256]{3,2,1,0:T(1,128)S(1)} %collective-permute-done.1, f32[2,16,1,256]{3,2,1,0:T(1,128)S(1)} %collective-permute-done, ...), kind=kLoop, calls=%fused_computation.87 | loop fusion | flops 4456448 | bytes 5575168 | tf_op jit(solution)/shard_map/mul | solution.py:54
  48.2 3.5 %collective-permute-start.8 = (f32[2,16,1,256]{3,2,1,0:T(1,128)S(1)}, f32[2,16,1,256]{3,2,1,0:T(1,128)S(1)}, u32[]{:S(2)}, u32[]{:S(2)}) collective-permute-start(f32[2,16,1,256]{3,2,1,0:T(1,128)S(1)} %get-tuple-element.15), channel_id=1, source_target_pairs={{16,0},{32,16},{48,32},{64,48},{80,64},{96,80},{112,96},{128,112},... | collective-permute-start | bytes 98312 | tf_op jit(solution)/shard_map/ppermute | solution.py:17
  51.7 3.8 %collective-permute-start.9 = (f32[2,16,1,256]{3,2,1,0:T(1,128)S(1)}, f32[2,16,1,256]{3,2,1,0:T(1,128)S(1)}, u32[]{:S(2)}, u32[]{:S(2)}) collective-permute-start(f32[2,16,1,256]{3,2,1,0:T(1,128)S(1)} %get-tuple-element.16), channel_id=1, source_target_pairs={{0,16},{16,32},{32,48},{48,64},{64,80},{80,96},{96,112},{112,128},... | collective-permute-start | bytes 98312 | tf_op jit(solution)/shard_map/ppermute | solution.py:15
  56.8 2.1 %collective-permute-start.10 = (f32[2,16,18,1]{3,2,1,0:T(8,128)S(1)}, f32[2,16,18,1]{3,2,1,0:T(8,128)S(1)}, u32[]{:S(2)}, u32[]{:S(2)}) collective-permute-start(f32[2,16,18,1]{3,2,1,0:T(8,128)S(1)} %get-tuple-element.11), channel_id=1, source_target_pairs={{1,0},{2,1},{3,2},{4,3},{5,4},{6,5},{7,6},{8,7},{9,8},{10,9},{11,1... | collective-permute-start | bytes 6920 | tf_op jit(solution)/shard_map/ppermute | solution.py:17
  58.8 3.5 %collective-permute-start.11 = (f32[2,16,18,1]{3,2,1,0:T(8,128)S(1)}, f32[2,16,18,1]{3,2,1,0:T(8,128)S(1)}, u32[]{:S(2)}, u32[]{:S(2)}) collective-permute-start(f32[2,16,18,1]{3,2,1,0:T(8,128)S(1)} %get-tuple-element.12), channel_id=1, source_target_pairs={{0,1},{1,2},{2,3},{3,4},{4,5},{5,6},{6,7},{7,8},{8,9},{9,10},{10,1... | collective-permute-start | bytes 6920 | tf_op jit(solution)/shard_map/ppermute | solution.py:15
  63.0 6.0 %collective-permute-done.10 = f32[2,16,18,1]{3,2,1,0:T(8,128)S(1)} collective-permute-done((f32[2,16,18,1]{3,2,1,0:T(8,128)S(1)}, f32[2,16,18,1]{3,2,1,0:T(8,128)S(1)}, u32[]{:S(2)}, u32[]{:S(2)}) %collective-permute-start.10) | collective-permute-done | bytes 2336 | tf_op jit(solution)/shard_map/ppermute | solution.py:17
  68.9 1.7 collective-permute-done.11
  70.7 1.3 fusion.7
  72.1 12.2 %collective-permute-start.12 = (f32[16,16,256]{2,1,0:T(8,128)S(1)}, f32[16,16,256]{2,1,0:T(8,128)S(1)}, u32[]{:S(2)}, u32[]{:S(2)}) collective-permute-start(f32[16,16,256]{2,1,0:T(8,128)S(1)} %broadcast_select_fusion), channel_id=1, source_target_pairs={{0,256},{256,0},{1,257},{257,1},{2,258},{258,2},{3,259},{259,3},{4... | collective-permute-start | bytes 786440 | tf_op jit(solution)/shard_map/ppermute | solution.py:106
  84.3 22.2 %collective-permute-done.12 = f32[16,16,256]{2,1,0:T(8,128)S(1)} collective-permute-done((f32[16,16,256]{2,1,0:T(8,128)S(1)}, f32[16,16,256]{2,1,0:T(8,128)S(1)}, u32[]{:S(2)}, u32[]{:S(2)}) %collective-permute-start.12) | collective-permute-done | bytes 262176 | tf_op jit(solution)/shard_map/ppermute | solution.py:106
  106.7 1.6 stack.2
  108.2 9.7 %all-to-all-start = ((bf16[16,16,16,256]{3,2,1,0:T(8,128)(2,1)}), bf16[16,16,16,256]{3,2,1,0:T(8,128)(2,1)S(1)}, u32[]{:S(2)}, u32[]{:S(2)}) async-start(bf16[16,16,16,256]{3,2,1,0:T(8,128)(2,1)} %stack.2), calls=%async_computation | async-start | bytes 4194304 | tf_op jit(solution)/shard_map/all_to_all | solution.py:109
  118.0 1.9 %select_maximum_fusion = f32[2,18,18,258]{3,2,1,0:T(8,128)S(1)} fusion(f32[2,16,18,1]{3,2,1,0:T(8,128)S(1)} %collective-permute-done.10, f32[2,16,18,1]{3,2,1,0:T(8,128)} %copy-done.2, f32[2,16,1,256]{3,2,1,0:T(1,128)S(1)} %collective-permute-done.8, f32[2,16,16,256]{3,2,1,0:T(8,128)S(1)} %get-tuple-element.7, f32[2,16,1,256]{3,2,1,0:T(1,128)S(1)} %collective-permute-done.9), kind=kLoop, calls=%fused_computation.4 | loop fusion | flops 2006208 | bytes 1263168 | tf_op jit(solution)/shard_map/concatenate | solution.py:13
  119.9 1.7 fusion.9
  121.6 22.2 %all-to-all-done = bf16[16,16,16,256]{3,2,1,0:T(8,128)(2,1)S(1)} async-done(((bf16[16,16,16,256]{3,2,1,0:T(8,128)(2,1)}), bf16[16,16,16,256]{3,2,1,0:T(8,128)(2,1)S(1)}, u32[]{:S(2)}, u32[]{:S(2)}) %all-to-all-start) | async-done | bytes 2097184 | tf_op jit(solution)/shard_map/all_to_all | solution.py:109
  143.9 2.5 %copy.18 = bf16[16,16,16,256]{3,2,1,0:T(8,128)(2,1)} copy(bf16[16,16,16,256]{3,1,0,2:T(8,128)(2,1)S(1)} %bitcast.50) | data formatting | bytes 4194304 | tf_op jit(solution)/shard_map/reshape | solution.py:108
  146.4 2.7 %reshape.73 = bf16[16,16,32,128,1]{3,2,1,0,4:T(8,128)(2,1)S(1)} reshape(bf16[16,16,16,256]{3,2,1,0:T(8,128)(2,1)} %copy.18) | data formatting | bytes 4194304 | tf_op jit(solution)/shard_map/reshape;reshape | solution.py:112
  150.8 11.0 %collective-permute-start.13 = (f32[16,16,256]{2,1,0:T(8,128)S(1)}, f32[16,16,256]{2,1,0:T(8,128)S(1)}, u32[]{:S(2)}, u32[]{:S(2)}) collective-permute-start(f32[16,16,256]{2,1,0:T(8,128)S(1)} %fusion.43), channel_id=1, source_target_pairs={{0,256},{256,0},{1,257},{257,1},{2,258},{258,2},{3,259},{259,3},{4... | collective-permute-start | bytes 786440 | tf_op jit(solution)/shard_map/ppermute | solution.py:121
  162.9 16.2 %collective-permute-done.13 = f32[16,16,256]{2,1,0:T(8,128)S(1)} collective-permute-done((f32[16,16,256]{2,1,0:T(8,128)S(1)}, f32[16,16,256]{2,1,0:T(8,128)S(1)}, u32[]{:S(2)}, u32[]{:S(2)}) %collective-permute-start.13) | collective-permute-done | bytes 262176 | tf_op jit(solution)/shard_map/ppermute | solution.py:121
  (88 shorter events, 11.8 us)
Async XLA Ops:
  0.6 149.0 %copy-start = (bf16[2,7,128,128]{3,2,1,0:T(8,128)(2,1)S(1)}, bf16[2,7,128,128]{3,2,1,0:T(8,128)(2,1)}, u32[]{:S(2)}) copy-start(bf16[2,7,128,128]{3,2,1,0:T(8,128)(2,1)} %param.18) | copy-start | bytes 1376260
  0.6 15.9 %copy-start.4 = (f32[16,16,256]{2,1,0:T(8,128)S(1)}, f32[16,16,256]{2,1,0:T(8,128)}, u32[]{:S(2)}) copy-start(f32[16,16,256]{2,1,0:T(8,128)} %param.12) | copy-start | bytes 786436
  0.7 15.6 %copy-start.22 = (s32[16,16,256]{2,1,0:T(8,128)S(1)}, s32[16,16,256]{2,1,0:T(8,128)}, u32[]{:S(2)}) copy-start(s32[16,16,256]{2,1,0:T(8,128)} %param.14) | copy-start | bytes 786436
  0.7 15.9 %copy-start.25 = (f32[2,2,8]{2,1,0:T(2,128)S(1)}, f32[2,2,8]{2,1,0:T(2,128)}, u32[]{:S(2)}) copy-start(f32[2,2,8]{2,1,0:T(2,128)} %param.16) | copy-start | bytes 388
  1.7 14.8 %collective-permute-start.2 = (f32[16,1,256]{2,1,0:T(1,128)S(1)}, f32[16,1,256]{2,1,0:T(1,128)S(1)}, u32[]{:S(2)}, u32[]{:S(2)}) collective-permute-start(f32[16,1,256]{2,1,0:T(1,128)S(1)} %get-tuple-element.29), channel_id=1, source_target_pairs={{0,16},{16,32},{32,48},{48,64},{64,80},{80,96},{96,112},{112,128},... | collective-permute-start | bytes 49160 | tf_op jit(solution)/shard_map/ppermute | solution.py:15
  5.9 10.7 %collective-permute-start.3 = (f32[16,1,256]{2,1,0:T(1,128)S(1)}, f32[16,1,256]{2,1,0:T(1,128)S(1)}, u32[]{:S(2)}, u32[]{:S(2)}) collective-permute-start(f32[16,1,256]{2,1,0:T(1,128)S(1)} %get-tuple-element.30), channel_id=1, source_target_pairs={{16,0},{32,16},{48,32},{64,48},{80,64},{96,80},{112,96},{128,112},... | collective-permute-start | bytes 49160 | tf_op jit(solution)/shard_map/ppermute | solution.py:17
  8.9 19.6 %collective-permute-start = (f32[2,16,1,256]{3,2,1,0:T(1,128)S(1)}, f32[2,16,1,256]{3,2,1,0:T(1,128)S(1)}, u32[]{:S(2)}, u32[]{:S(2)}) collective-permute-start(f32[2,16,1,256]{3,2,1,0:T(1,128)S(1)} %get-tuple-element.19), channel_id=1, source_target_pairs={{16,0},{32,16},{48,32},{64,48},{80,64},{96,80},{112,96},{128,112},... | collective-permute-start | bytes 98312 | tf_op jit(solution)/shard_map/ppermute | solution.py:17
  11.0 17.5 %collective-permute-start.1 = (f32[2,16,1,256]{3,2,1,0:T(1,128)S(1)}, f32[2,16,1,256]{3,2,1,0:T(1,128)S(1)}, u32[]{:S(2)}, u32[]{:S(2)}) collective-permute-start(f32[2,16,1,256]{3,2,1,0:T(1,128)S(1)} %get-tuple-element.20), channel_id=1, source_target_pairs={{0,16},{16,32},{32,48},{48,64},{64,80},{80,96},{96,112},{112,128},... | collective-permute-start | bytes 98312 | tf_op jit(solution)/shard_map/ppermute | solution.py:15
  16.7 11.8 %copy-start.1 = (f32[2,16,16,256]{3,2,1,0:T(8,128)S(1)}, f32[2,16,16,256]{3,2,1,0:T(8,128)}, u32[]{:S(2)}) copy-start(f32[2,16,16,256]{3,2,1,0:T(8,128)} %param.10) | copy-start | bytes 1572868
  16.8 8.4 %collective-permute-start.4 = (f32[16,18,1]{2,1,0:T(8,128)S(1)}, f32[16,18,1]{2,1,0:T(8,128)S(1)}, u32[]{:S(2)}, u32[]{:S(2)}) collective-permute-start(f32[16,18,1]{2,1,0:T(8,128)S(1)} %get-tuple-element.22), channel_id=1, source_target_pairs={{0,1},{1,2},{2,3},{3,4},{4,5},{5,6},{6,7},{7,8},{8,9},{9,10},{10,1... | collective-permute-start | bytes 3464 | tf_op jit(solution)/shard_map/ppermute | solution.py:15
  19.8 8.2 %collective-permute-start.5 = (f32[16,18,1]{2,1,0:T(8,128)S(1)}, f32[16,18,1]{2,1,0:T(8,128)S(1)}, u32[]{:S(2)}, u32[]{:S(2)}) collective-permute-start(f32[16,18,1]{2,1,0:T(8,128)S(1)} %get-tuple-element.21), channel_id=1, source_target_pairs={{1,0},{2,1},{3,2},{4,3},{5,4},{6,5},{7,6},{8,7},{9,8},{10,9},{11,1... | collective-permute-start | bytes 3464 | tf_op jit(solution)/shard_map/ppermute | solution.py:17
  28.8 13.0 %collective-permute-start.6 = (f32[2,16,18,1]{3,2,1,0:T(8,128)S(1)}, f32[2,16,18,1]{3,2,1,0:T(8,128)S(1)}, u32[]{:S(2)}, u32[]{:S(2)}) collective-permute-start(f32[2,16,18,1]{3,2,1,0:T(8,128)S(1)} %get-tuple-element.14), channel_id=1, source_target_pairs={{0,1},{1,2},{2,3},{3,4},{4,5},{5,6},{6,7},{7,8},{8,9},{9,10},{10,1... | collective-permute-start | bytes 6920 | tf_op jit(solution)/shard_map/ppermute | solution.py:15
  33.7 11.9 %collective-permute-start.7 = (f32[2,16,18,1]{3,2,1,0:T(8,128)S(1)}, f32[2,16,18,1]{3,2,1,0:T(8,128)S(1)}, u32[]{:S(2)}, u32[]{:S(2)}) collective-permute-start(f32[2,16,18,1]{3,2,1,0:T(8,128)S(1)} %get-tuple-element.13), channel_id=1, source_target_pairs={{1,0},{2,1},{3,2},{4,3},{5,4},{6,5},{7,6},{8,7},{9,8},{10,9},{11,1... | collective-permute-start | bytes 6920 | tf_op jit(solution)/shard_map/ppermute | solution.py:17
  36.2 10.1 %copy-start.5 = (f32[16,16,256]{2,1,0:T(8,128)}, f32[16,16,256]{2,1,0:T(8,128)S(1)}, u32[]{:S(2)}) copy-start(f32[16,16,256]{2,1,0:T(8,128)S(1)} %get-tuple-element.23) | copy-start | bytes 786436
  36.2 10.1 %copy-start.7 = (f32[16,16,256]{2,1,0:T(8,128)}, f32[16,16,256]{2,1,0:T(8,128)S(1)}, u32[]{:S(2)}) copy-start(f32[16,16,256]{2,1,0:T(8,128)S(1)} %get-tuple-element.24) | copy-start | bytes 786436
  36.2 10.1 %copy-start.9 = (f32[16,16,256]{2,1,0:T(8,128)}, f32[16,16,256]{2,1,0:T(8,128)S(1)}, u32[]{:S(2)}) copy-start(f32[16,16,256]{2,1,0:T(8,128)S(1)} %get-tuple-element.25) | copy-start | bytes 786436
  36.2 10.1 %copy-start.11 = (f32[16,16,256]{2,1,0:T(8,128)}, f32[16,16,256]{2,1,0:T(8,128)S(1)}, u32[]{:S(2)}) copy-start(f32[16,16,256]{2,1,0:T(8,128)S(1)} %get-tuple-element.26) | copy-start | bytes 786436
  36.2 10.1 %copy-start.13 = (f32[16,16,256]{2,1,0:T(8,128)}, f32[16,16,256]{2,1,0:T(8,128)S(1)}, u32[]{:S(2)}) copy-start(f32[16,16,256]{2,1,0:T(8,128)S(1)} %get-tuple-element.27) | copy-start | bytes 786436
  36.2 10.1 %copy-start.15 = (f32[16,16,256]{2,1,0:T(8,128)}, f32[16,16,256]{2,1,0:T(8,128)S(1)}, u32[]{:S(2)}) copy-start(f32[16,16,256]{2,1,0:T(8,128)S(1)} %get-tuple-element.28) | copy-start | bytes 786436
  48.2 7.3 %collective-permute-start.8 = (f32[2,16,1,256]{3,2,1,0:T(1,128)S(1)}, f32[2,16,1,256]{3,2,1,0:T(1,128)S(1)}, u32[]{:S(2)}, u32[]{:S(2)}) collective-permute-start(f32[2,16,1,256]{3,2,1,0:T(1,128)S(1)} %get-tuple-element.15), channel_id=1, source_target_pairs={{16,0},{32,16},{48,32},{64,48},{80,64},{96,80},{112,96},{128,112},... | collective-permute-start | bytes 98312 | tf_op jit(solution)/shard_map/ppermute | solution.py:17
  51.7 4.8 %collective-permute-start.9 = (f32[2,16,1,256]{3,2,1,0:T(1,128)S(1)}, f32[2,16,1,256]{3,2,1,0:T(1,128)S(1)}, u32[]{:S(2)}, u32[]{:S(2)}) collective-permute-start(f32[2,16,1,256]{3,2,1,0:T(1,128)S(1)} %get-tuple-element.16), channel_id=1, source_target_pairs={{0,16},{16,32},{32,48},{48,64},{64,80},{80,96},{96,112},{112,128},... | collective-permute-start | bytes 98312 | tf_op jit(solution)/shard_map/ppermute | solution.py:15
  55.5 6.9 %copy-start.17 = (bf16[2,2,16,16,256]{4,3,2,1,0:T(8,128)(2,1)S(1)}, bf16[2,2,16,16,256]{4,3,2,1,0:T(8,128)(2,1)}, u32[]{:S(2)}) copy-start(bf16[2,2,16,16,256]{4,3,2,1,0:T(8,128)(2,1)} %param.11) | copy-start | bytes 1572868
  56.8 13.9 %copy-start.19 = (f32[2,16,16,256]{3,2,1,0:T(8,128)S(1)}, f32[2,16,16,256]{3,2,1,0:T(8,128)}, u32[]{:S(2)}) copy-start(f32[2,16,16,256]{3,2,1,0:T(8,128)} %get-tuple-element.8) | copy-start | bytes 1572868
  56.8 12.2 %collective-permute-start.10 = (f32[2,16,18,1]{3,2,1,0:T(8,128)S(1)}, f32[2,16,18,1]{3,2,1,0:T(8,128)S(1)}, u32[]{:S(2)}, u32[]{:S(2)}) collective-permute-start(f32[2,16,18,1]{3,2,1,0:T(8,128)S(1)} %get-tuple-element.11), channel_id=1, source_target_pairs={{1,0},{2,1},{3,2},{4,3},{5,4},{6,5},{7,6},{8,7},{9,8},{10,9},{11,1... | collective-permute-start | bytes 6920 | tf_op jit(solution)/shard_map/ppermute | solution.py:17
  58.8 11.8 %collective-permute-start.11 = (f32[2,16,18,1]{3,2,1,0:T(8,128)S(1)}, f32[2,16,18,1]{3,2,1,0:T(8,128)S(1)}, u32[]{:S(2)}, u32[]{:S(2)}) collective-permute-start(f32[2,16,18,1]{3,2,1,0:T(8,128)S(1)} %get-tuple-element.12), channel_id=1, source_target_pairs={{0,1},{1,2},{2,3},{3,4},{4,5},{5,6},{6,7},{7,8},{8,9},{9,10},{10,1... | collective-permute-start | bytes 6920 | tf_op jit(solution)/shard_map/ppermute | solution.py:15
  70.6 37.6 %copy-start.2 = (f32[2,16,18,1]{3,2,1,0:T(8,128)}, f32[2,16,18,1]{3,2,1,0:T(8,128)S(1)}, u32[]{:S(2)}) copy-start(f32[2,16,18,1]{3,2,1,0:T(8,128)S(1)} %collective-permute-done.11) | copy-start | bytes 6916
  72.1 34.5 %collective-permute-start.12 = (f32[16,16,256]{2,1,0:T(8,128)S(1)}, f32[16,16,256]{2,1,0:T(8,128)S(1)}, u32[]{:S(2)}, u32[]{:S(2)}) collective-permute-start(f32[16,16,256]{2,1,0:T(8,128)S(1)} %broadcast_select_fusion), channel_id=1, source_target_pairs={{0,256},{256,0},{1,257},{257,1},{2,258},{258,2},{3,259},{259,3},{4... | collective-permute-start | bytes 786440 | tf_op jit(solution)/shard_map/ppermute | solution.py:106
  108.2 35.6 %all-to-all-start = ((bf16[16,16,16,256]{3,2,1,0:T(8,128)(2,1)}), bf16[16,16,16,256]{3,2,1,0:T(8,128)(2,1)S(1)}, u32[]{:S(2)}, u32[]{:S(2)}) async-start(bf16[16,16,16,256]{3,2,1,0:T(8,128)(2,1)} %stack.2), calls=%async_computation | async-start | bytes 4194304 | tf_op jit(solution)/shard_map/all_to_all | solution.py:109
  117.9 2.0 %copy-start.6 = (f32[16,16,256]{2,1,0:T(8,128)S(1)}, f32[16,16,256]{2,1,0:T(8,128)}, u32[]{:S(2)}) copy-start(f32[16,16,256]{2,1,0:T(8,128)} %copy-done.5) | copy-start | bytes 786436
  117.9 2.0 %copy-start.8 = (f32[16,16,256]{2,1,0:T(8,128)S(1)}, f32[16,16,256]{2,1,0:T(8,128)}, u32[]{:S(2)}) copy-start(f32[16,16,256]{2,1,0:T(8,128)} %copy-done.7) | copy-start | bytes 786436
  146.4 2.7 %copy-start.24 = (s32[2,7]{1,0:T(2,128)S(1)}, s32[2,7]{1,0:T(2,128)}, u32[]{:S(2)}) copy-start(s32[2,7]{1,0:T(2,128)} %param.19) | copy-start | bytes 172
  150.8 28.4 %collective-permute-start.13 = (f32[16,16,256]{2,1,0:T(8,128)S(1)}, f32[16,16,256]{2,1,0:T(8,128)S(1)}, u32[]{:S(2)}, u32[]{:S(2)}) collective-permute-start(f32[16,16,256]{2,1,0:T(8,128)S(1)} %fusion.43), channel_id=1, source_target_pairs={{0,256},{256,0},{1,257},{257,1},{2,258},{258,2},{3,259},{259,3},{4... | collective-permute-start | bytes 786440 | tf_op jit(solution)/shard_map/ppermute | solution.py:121
  (9 other events, 14.8 us)
